TPU v7x, 512 devices: a whole 4x8x8 slice. The times are simulated.
512 devices in a mesh: row: 8 (over z), col: 16 (over y, core), vox: 4 (over x).
Axes of the slice: x: 4, y: 8, z: 8, core: 2. Of those that a mesh axis runs over, the one named last changes fastest.
Arguments:
- panel_top: bfloat16 [1024, 1024], P('row', ('col', 'vox')), may hold values from -0.059814453 to 0.059814453
- panel_low: bfloat16 [8192, 1024], P('row', ('col', 'vox')), may hold values from -1.1953125 to 1.1953125
- panel_next: bfloat16 [8192, 1024], P('row', ('col', 'vox')), may hold values from -1.1953125 to 1.1953125
- gram_rest: bfloat16 [8192, 8192], P('row', ('col', 'vox')), may hold values from -18 to 18
- inverses: bfloat16 [2, 1024, 1024], P(None, 'row'), as said below
- right_top: bfloat16 [2, 1024, 8192], P(None, None, ('col', 'vox')), may hold values from -1.796875 to 1.796875
- right_low: bfloat16 [8192, 8192], P('row', ('col', 'vox')), may hold values from -24 to 24
Outputs:
- factor: bfloat16 [2, 8192, 1024], P(None, 'row', ('col', 'vox'))
- solved: bfloat16 [2, 1024, 8192], P(None, None, ('col', 'vox'))
- trailing: float32 [8192, 8192], P('row', ('col', 'vox'))
- residual: float32 [8192, 8192], P('row', ('col', 'vox'))
Inputs may be any that keep to these rules, and one draw needn't show every extreme that they name: Each inverses[k] is lower triangular with diagonal entries from 1 to 2.
All inputs are finite; a program needn't handle non-finite values.
Results may differ from a plain program's by a relative error of at most 0.0057.
Values may be sent and summed in bfloat16 or wider, within the bound.
No kernel may reach another device: no remote copies, remote signals or barrier semaphores. Data moves between devices by JAX's collectives and lax.ppermute only.
A program may use at most 64 MiB of HBM per device.

v0:
```python
import jax
import jax.numpy as jnp
import numpy as np
from jax import lax
from jax.sharding import Mesh
from jax.sharding import PartitionSpec as P


def contract(left, right, dims):
    return lax.dot_general(left, right, (dims, ((), ())), preferred_element_type=jnp.float32)


def gather_small(block, axis, size):
    out = lax.all_to_all(jnp.tile(block, (size, 1)), axis, 0, 0, tiled=True)
    return out.reshape((size,) + block.shape)


def per_device(sizes, panel_top, panel_low, panel_next, gram_rest, inverses, right_top, right_low):
    rows, ys, cores, voxes = sizes
    axes = ("row", "y", "core", "vox")
    order = np.arange(rows * ys * cores * voxes).reshape(sizes)
    swap = list(zip(order.ravel().tolist(), order.transpose(1, 0, 2, 3).ravel().tolist()))
    y = lax.axis_index("y")
    core = lax.axis_index("core")
    vox = lax.axis_index("vox")
    width = panel_low.shape[1]
    rest_cols = gram_rest.shape[1]
    bf16 = jnp.bfloat16
    whole = lax.all_gather(inverses, "row", axis=1, tiled=True)
    top = gather_small(panel_top.T, "row", rows).transpose(1, 0, 2).reshape(width, -1)
    panels = jnp.stack([top, panel_low.T, panel_next.T])
    panels = lax.all_gather(panels, ("y", "core", "vox"), axis=1, tiled=True)
    low = panels[0:2].transpose(1, 0, 2).reshape(panels.shape[1], -1)
    first = contract(whole[0], low, ((1,), (0,))).astype(bf16)
    first_top, first_low = (first[:, : panels.shape[2]], first[:, panels.shape[2] :])
    updated = (panels[2].astype(jnp.float32) - contract(first_top, first_low, ((0,), (0,)))).astype(
        bf16
    )
    second_low = contract(whole[1], updated, ((1,), (0,))).astype(bf16)
    start = (core * voxes + vox) * rest_cols
    first_rows = lax.ppermute(lax.dynamic_slice_in_dim(first_low, start, rest_cols, 1), axes, swap)
    second_rows = lax.ppermute(
        lax.dynamic_slice_in_dim(second_low, start, rest_cols, 1), axes, swap
    )
    first_solve = contract(whole[0], right_top[0], ((1,), (0,))).astype(bf16)
    top_new = (
        right_top[1].astype(jnp.float32) - contract(first_top, first_solve, ((0,), (0,)))
    ).astype(bf16)
    second_solve = contract(whole[1], top_new, ((1,), (0,))).astype(bf16)
    residual = (
        right_low.astype(jnp.float32)
        - contract(first_low, first_solve, ((0,), (0,)))
        - contract(second_low, second_solve, ((0,), (0,)))
    )
    trailing = (
        gram_rest.astype(jnp.float32)
        - contract(first_low, first_rows, ((0,), (0,)))
        - contract(second_low, second_rows, ((0,), (0,)))
    )
    own = ((y * cores + core) * voxes + vox) * width
    factor = jnp.stack(
        [
            lax.dynamic_slice_in_dim(first_low, own, width, 0).T,
            lax.dynamic_slice_in_dim(second_low, own, width, 0).T,
        ]
    )
    solved = jnp.stack([first_solve, second_solve])
    return (factor, solved, trailing, residual)


def solution(mesh):
    cores = 2
    sizes = (mesh.shape["row"], mesh.shape["col"] // cores, cores, mesh.shape["vox"])
    split = Mesh(mesh.devices.reshape(sizes), ("row", "y", "core", "vox"))
    cols = ("y", "core", "vox")
    in_specs = (
        P("row", cols),
        P("row", cols),
        P("row", cols),
        P("row", cols),
        P(None, "row", None),
        P(None, None, cols),
        P("row", cols),
    )
    out_specs = (P(None, "row", cols), P(None, None, cols), P("row", cols), P("row", cols))

    def body(*args):
        return per_device(sizes, *args)

    return jax.shard_map(body, mesh=split, in_specs=in_specs, out_specs=out_specs, check_vma=False)
```

profile of v0, /device:TPU:16, one launch (start us, length us, event | category | flops | bytes accessed | tf_op | source)
XLA Modules:
  0.0 259.9 jit_solution(18153763955404550325)
XLA Ops:
  8.6 18.1 %all_to_all.6 = bf16[8,16,128]{2,1,0:T(8,128)(2,1)S(1)} all-to-all(bf16[8,16,128]{2,1,0:T(8,128)(2,1)S(1)} %tile.2), channel_id=1, replica_groups=mesh['row'=8,'y'=8,'core'=2,'vox'=4] {'row'}, dimensions={0} | all-to-all | bytes 65536 | tf_op jit(solution)/shard_map/all_to_all | solution.py:14
  26.8 1.4 pad_maximum_fusion.1
  28.3 44.6 %all-gather.5.cloned.1.call-done = bf16[2,1024,1024]{2,1,0:T(8,128)(2,1)} async-done(((bf16[2,128,1024]{2,1,0:T(8,128)(2,1)}), bf16[2,1024,1024]{2,1,0:T(8,128)(2,1)}) %all-gather.5.cloned.1.call-update) | async-done | bytes 4194320 | tf_op jit(solution)/shard_map/all_gather | solution.py:29
  72.9 2.3 fusion.17
  75.2 85.2 %all-gather.3.cloned.1.call-done = bf16[3,1024,1024]{2,1,0:T(8,128)(2,1)} async-done(((bf16[3,16,1024]{2,1,0:T(8,128)(2,1)}), bf16[3,1024,1024]{2,1,0:T(8,128)(2,1)}) %all-gather.3.cloned.1.call-update) | async-done | bytes 6291472 | tf_op jit(solution)/shard_map/all_gather | solution.py:32
  160.4 4.7 %slice.34 = bf16[2,1024,1024]{2,1,0:T(8,128)(2,1)} slice(bf16[3,1024,1024]{2,1,0:T(8,128)(2,1)} %all-gather.3.cloned.1.call-done), slice={[0:2], [0:1024], [0:1024]} | slice | bytes 8388608 | tf_op jit(solution)/shard_map/slice | solution.py:33
  165.1 6.2 %copy.22 = bf16[2,1024,1024]{1,2,0:T(8,128)(2,1)} copy(bf16[2,1024,1024]{2,1,0:T(8,128)(2,1)} %slice.34) | data formatting | bytes 8388608
  171.3 7.4 %convert_bitcast_fusion = bf16[1024,2048]{1,0:T(8,128)(2,1)S(1)} fusion(bf16[1024,2048]{0,1:T(8,128)(2,1)} %bitcast.62, bf16[2,1024,1024]{2,1,0:T(8,128)(2,1)} %all-gather.5.cloned.1.call-done), kind=kOutput, calls=%fused_computation.2 | convolution fusion | flops 4297064448 | bytes 10485760 | tf_op jit(solution)/shard_map/dot_general | solution.py:10
  178.7 2.0 copy-done
  180.7 1.5 slice.36
  182.2 8.0 %fusion.3 = bf16[1024,1024]{0,1:T(8,128)(2,1)S(1)} fusion(bf16[3,1024,1024]{2,1,0:T(8,128)(2,1)} %all-gather.3.cloned.1.call-done, bf16[2,1024,1024]{2,1,0:T(8,128)(2,1)} %all-gather.5.cloned.1.call-done, bf16[1024,2048]{1,0:T(8,128)(2,1)} %copy-done), kind=kOutput, calls=%fused_computation.7 | convolution fusion | flops 4299161600 | bytes 10485760 | tf_op jit(solution)/shard_map/dot_general | solution.py:10
  190.2 0.8 dynamic-slice_bitcast_fusion.2
  191.0 0.8 dynamic-slice_bitcast_fusion
  191.8 1.0 constant_dynamic-slice_fusion
  192.8 5.5 %collective-permute-start.1 = (bf16[1024,128]{1,0:T(8,128)(2,1)}, bf16[1024,128]{1,0:T(8,128)(2,1)S(1)}, u32[]{:S(2)}, u32[]{:S(2)}) collective-permute-start(bf16[1024,128]{1,0:T(8,128)(2,1)} %dynamic-slice_bitcast_fusion), channel_id=1, source_target_pairs={{0,0},{1,1},{2,2},{3,3},{4,4},{5,5},{6,6},{7,7},{8,64},{9,65},{10,... | collective-permute-start | bytes 786440 | tf_op jit(solution)/shard_map/ppermute | solution.py:42
  198.2 3.2 %collective-permute-start = (bf16[1024,128]{1,0:T(8,128)(2,1)S(1)}, bf16[1024,128]{1,0:T(8,128)(2,1)}, u32[]{:S(2)}, u32[]{:S(2)}) collective-permute-start(bf16[1024,128]{1,0:T(8,128)(2,1)S(1)} %constant_dynamic-slice_fusion), channel_id=1, source_target_pairs={{0,0},{1,1},{2,2},{3,3},{4,4},{5,5},{6,6},{7,7},{8,64},{9,65},{10,... | collective-permute-start | bytes 786440 | tf_op jit(solution)/shard_map/ppermute | solution.py:41
  202.1 2.3 convolution_subtract_fusion.1
  204.5 4.5 %fusion.16 = bf16[128,1024]{0,1:T(8,128)(2,1)S(1)} fusion(bf16[2,1024,1024]{2,1,0:T(8,128)(2,1)} %all-gather.5.cloned.1.call-done, bf16[1024,128]{1,0:T(8,128)(2,1)} %copy-done.2, bf16[1024,2048]{1,0:T(8,128)(2,1)} %copy-done, bf16[2,1024,128]{2,1,0:T(8,128)(2,1)} %param.12), kind=kOutput, calls=%fused_computation.19 | convolution fusion | flops 537395200 | bytes 4980736 | tf_op jit(solution)/shard_map/dot_general | solution.py:10
  209.0 1.8 pad_maximum_fusion
  210.8 1.5 convolution_subtract_fusion
  212.3 33.1 %collective-permute-done.1 = bf16[1024,128]{1,0:T(8,128)(2,1)S(1)} collective-permute-done((bf16[1024,128]{1,0:T(8,128)(2,1)}, bf16[1024,128]{1,0:T(8,128)(2,1)S(1)}, u32[]{:S(2)}, u32[]{:S(2)}) %collective-permute-start.1) | collective-permute-done | bytes 262176 | tf_op jit(solution)/shard_map/ppermute | solution.py:42
  245.4 0.7 fusion.36
  246.2 4.4 %collective-permute-done = bf16[1024,128]{1,0:T(8,128)(2,1)} collective-permute-done((bf16[1024,128]{1,0:T(8,128)(2,1)S(1)}, bf16[1024,128]{1,0:T(8,128)(2,1)}, u32[]{:S(2)}, u32[]{:S(2)}) %collective-permute-start) | collective-permute-done | bytes 262176 | tf_op jit(solution)/shard_map/ppermute | solution.py:41
  250.6 2.5 fusion.15
  (16 shorter events, 2.2 us)
Async XLA Ops:
  7.2 65.7 %all-gather.5.cloned.1.call-start = ((), (), s32[]{:S(2)}) async-start(), calls=%async_computation.2 | async-start | bytes 4718592 | tf_op jit(solution)/shard_map/all_gather | solution.py:29
  7.9 152.5 %all-gather.3.cloned.1.call-start = ((), (), s32[]{:S(2)}) async-start(), calls=%async_computation.1 | async-start | bytes 6389760 | tf_op jit(solution)/shard_map/all_gather | solution.py:32
  75.2 127.0 %copy-start.2 = (bf16[1024,128]{1,0:T(8,128)(2,1)}, bf16[1024,128]{1,0:T(8,128)(2,1)S(1)}, u32[]{:S(2)}) copy-start(bf16[1024,128]{1,0:T(8,128)(2,1)S(1)} %fusion.17) | copy-start | bytes 786436
  178.7 2.1 copy-start
  192.8 52.7 %collective-permute-start.1 = (bf16[1024,128]{1,0:T(8,128)(2,1)}, bf16[1024,128]{1,0:T(8,128)(2,1)S(1)}, u32[]{:S(2)}, u32[]{:S(2)}) collective-permute-start(bf16[1024,128]{1,0:T(8,128)(2,1)} %dynamic-slice_bitcast_fusion), channel_id=1, source_target_pairs={{0,0},{1,1},{2,2},{3,3},{4,4},{5,5},{6,6},{7,7},{8,64},{9,65},{10,... | collective-permute-start | bytes 786440 | tf_op jit(solution)/shard_map/ppermute | solution.py:42
  198.2 52.3 %collective-permute-start = (bf16[1024,128]{1,0:T(8,128)(2,1)S(1)}, bf16[1024,128]{1,0:T(8,128)(2,1)}, u32[]{:S(2)}, u32[]{:S(2)}) collective-permute-start(bf16[1024,128]{1,0:T(8,128)(2,1)S(1)} %constant_dynamic-slice_fusion), channel_id=1, source_target_pairs={{0,0},{1,1},{2,2},{3,3},{4,4},{5,5},{6,6},{7,7},{8,64},{9,65},{10,... | collective-permute-start | bytes 786440 | tf_op jit(solution)/shard_map/ppermute | solution.py:41
  210.8 39.7 %copy-start.1 = (bf16[1024,2048]{1,0:T(8,128)(2,1)S(1)}, bf16[1024,2048]{1,0:T(8,128)(2,1)}, u32[]{:S(2)}) copy-start(bf16[1024,2048]{1,0:T(8,128)(2,1)} %copy-done) | copy-start | bytes 12582916
  210.8 39.7 %copy-start.3 = (bf16[1024,128]{1,0:T(8,128)(2,1)S(1)}, bf16[1024,128]{1,0:T(8,128)(2,1)}, u32[]{:S(2)}) copy-start(bf16[1024,128]{1,0:T(8,128)(2,1)} %param.10) | copy-start | bytes 786436
Sparse Core Ops, SparseCore 0:
  10.1 62.7 all-gather.4
  76.8 83.5 all-gather.2
where the time goes:
time: 261 us; the launch traced here: 260 us
  waiting for transfers between devices  168 us (64%)
  matrix products  29.4 us (11%)
  blocking collectives  18.1 us (7%)
  local copies, waits for them, and re-layouts  17.6 us (7%)
  between operations  14.1 us (5%)
  starting transfers between devices  8.8 us (3%)
  other arithmetic  3.86 us (1%)
    all_gather x1, waiting for transfers between devices, per_device(): panels = lax.all_gather(panels, ('y', 'core', 'vox'), axis=1, tiled=True)  85.2 us
    all_gather x1, waiting for transfers between devices, per_device(): whole = lax.all_gather(inverses, 'row', axis=1, tiled=True)  44.6 us
    ppermute x1, waiting for transfers between devices, per_device(): lax.ppermute(lax.dynamic_slice_in_dim(second_low, start, rest_cols, 1), a...  33.1 us
    dot_general x8, matrix products, contract(): lax.dot_general(left, right, (dims, ((), ())), preferred_element_type=jnp...  29.4 us
    all_to_all x1, blocking collectives, gather_small(): out = lax.all_to_all(jnp.tile(block, (size, 1)), axis, 0, 0, tiled=True)  18.1 us
    unnamed x9, local copies, waits for them, and re-layouts  8.24 us
    ppermute x1, starting transfers between devices, per_device(): lax.ppermute(lax.dynamic_slice_in_dim(second_low, start, rest_cols, 1), a...  5.48 us
  transfers between devices with their start and end apart: 4, of which 4 were waited for; matrix products, arithmetic and copies ran while one was open for 6% of the time, Pallas kernels for 0%

commit v1 on v0

--- a/solution.py
+++ b/solution.py
@@ -26,7 +26,12 @@
     width = panel_low.shape[1]
     rest_cols = gram_rest.shape[1]
     bf16 = jnp.bfloat16
-    whole = lax.all_gather(inverses, "row", axis=1, tiled=True)
+    ring = [inverses]
+    for hop in range(7):
+        ring.append(lax.ppermute(ring[-1], "row", [(dev, (dev + 1) % 8) for dev in range(8)]))
+    whole = jnp.roll(
+        jnp.concatenate(ring[::-1], axis=1), (lax.axis_index("row") + 1) * ring[0].shape[1], axis=1
+    )
     top = gather_small(panel_top.T, "row", rows).transpose(1, 0, 2).reshape(width, -1)
     panels = jnp.stack([top, panel_low.T, panel_next.T])
     panels = lax.all_gather(panels, ("y", "core", "vox"), axis=1, tiled=True)

time: 261 us -> 223 us (0.85)
  the two profiles are of different devices: /device:TPU:16 before, /device:TPU:23 now
where the time goes in v1:
time: 223 us
  waiting for transfers between devices  118 us (53%)
  matrix products  25.2 us (11%)
  local copies, waits for them, and re-layouts  24 us (11%)
  starting transfers between devices  21.9 us (10%)
  blocking collectives  16.7 us (7%)
  between operations  14.4 us (6%)
  other arithmetic  2.91 us (1%)
    ppermute x7, waiting for transfers between devices, per_device(): lax.ppermute(ring[-1], 'row', [(dev, (dev + 1) % 8) for dev in range(8)])  74.7 us
    ppermute x1, waiting for transfers between devices, per_device(): lax.ppermute(lax.dynamic_slice_in_dim(second_low, start, rest_cols, 1), a...  37.9 us
    dot_general x8, matrix products, contract(): lax.dot_general(left, right, (dims, ((), ())), preferred_element_type=jnp...  25.2 us
    all_to_all x1, blocking collectives, gather_small(): out = lax.all_to_all(jnp.tile(block, (size, 1)), axis, 0, 0, tiled=True)  16.7 us
    unnamed x32, local copies, waits for them, and re-layouts  15.2 us
    ppermute x7, starting transfers between devices, per_device(): lax.ppermute(ring[-1], 'row', [(dev, (dev + 1) % 8) for dev in range(8)])  13.6 us
    ppermute x1, starting transfers between devices, per_device(): lax.ppermute(lax.dynamic_slice_in_dim(first_low, start, rest_cols, 1), ax...  6.06 us
    ppermute x1, waiting for transfers between devices, per_device(): lax.ppermute(lax.dynamic_slice_in_dim(first_low, start, rest_cols, 1), ax...  4.88 us
  transfers between devices with their start and end apart: 10, of which 9 were waited for; matrix products, arithmetic and copies ran while one was open for 5% of the time, Pallas kernels for 0%

profile of v1, /device:TPU:23, one launch (start us, length us, event | category | flops | bytes accessed | tf_op | source)
XLA Modules:
  0.0 222.6 jit_solution(862702829850397542)
XLA Ops:
  8.0 16.7 %all_to_all.6 = bf16[8,16,128]{2,1,0:T(8,128)(2,1)S(1)} all-to-all(bf16[8,16,128]{2,1,0:T(8,128)(2,1)S(1)} %tile.2), channel_id=1, replica_groups=mesh['row'=8,'y'=8,'core'=2,'vox'=4] {'row'}, dimensions={0} | all-to-all | bytes 65536 | tf_op jit(solution)/shard_map/all_to_all | solution.py:14
  26.2 2.2 collective-permute-start
  28.4 12.4 %collective-permute-done = bf16[2,128,1024]{2,1,0:T(8,128)(2,1)S(1)} collective-permute-done((bf16[2,128,1024]{2,1,0:T(8,128)(2,1)}, bf16[2,128,1024]{2,1,0:T(8,128)(2,1)S(1)}, u32[]{:S(2)}, u32[]{:S(2)}) %collective-permute-start) | collective-permute-done | bytes 524320 | tf_op jit(solution)/shard_map/ppermute | solution.py:31
  40.8 1.9 collective-permute-start.1
  42.7 11.7 %collective-permute-done.1 = bf16[2,128,1024]{2,1,0:T(8,128)(2,1)S(1)} collective-permute-done((bf16[2,128,1024]{2,1,0:T(8,128)(2,1)S(1)}, bf16[2,128,1024]{2,1,0:T(8,128)(2,1)S(1)}, u32[]{:S(2)}, u32[]{:S(2)}) %collective-permute-start.1) | collective-permute-done | bytes 524320 | tf_op jit(solution)/shard_map/ppermute | solution.py:31
  54.4 1.9 collective-permute-start.2
  56.3 10.7 %collective-permute-done.2 = bf16[2,128,1024]{2,1,0:T(8,128)(2,1)S(1)} collective-permute-done((bf16[2,128,1024]{2,1,0:T(8,128)(2,1)S(1)}, bf16[2,128,1024]{2,1,0:T(8,128)(2,1)S(1)}, u32[]{:S(2)}, u32[]{:S(2)}) %collective-permute-start.2) | collective-permute-done | bytes 524320 | tf_op jit(solution)/shard_map/ppermute | solution.py:31
  67.0 1.9 collective-permute-start.3
  69.0 9.8 %collective-permute-done.3 = bf16[2,128,1024]{2,1,0:T(8,128)(2,1)S(1)} collective-permute-done((bf16[2,128,1024]{2,1,0:T(8,128)(2,1)S(1)}, bf16[2,128,1024]{2,1,0:T(8,128)(2,1)S(1)}, u32[]{:S(2)}, u32[]{:S(2)}) %collective-permute-start.3) | collective-permute-done | bytes 524320 | tf_op jit(solution)/shard_map/ppermute | solution.py:31
  80.7 9.2 %collective-permute-done.4 = bf16[2,128,1024]{2,1,0:T(8,128)(2,1)S(1)} collective-permute-done((bf16[2,128,1024]{2,1,0:T(8,128)(2,1)S(1)}, bf16[2,128,1024]{2,1,0:T(8,128)(2,1)S(1)}, u32[]{:S(2)}, u32[]{:S(2)}) %collective-permute-start.4) | collective-permute-done | bytes 524320 | tf_op jit(solution)/shard_map/ppermute | solution.py:31
  89.9 1.9 collective-permute-start.5
  91.8 10.0 %collective-permute-done.5 = bf16[2,128,1024]{2,1,0:T(8,128)(2,1)} collective-permute-done((bf16[2,128,1024]{2,1,0:T(8,128)(2,1)S(1)}, bf16[2,128,1024]{2,1,0:T(8,128)(2,1)}, u32[]{:S(2)}, u32[]{:S(2)}) %collective-permute-start.5) | collective-permute-done | bytes 524320 | tf_op jit(solution)/shard_map/ppermute | solution.py:31
  101.8 1.9 collective-permute-start.6
  103.7 10.9 %collective-permute-done.6 = bf16[2,128,1024]{2,1,0:T(8,128)(2,1)} collective-permute-done((bf16[2,128,1024]{2,1,0:T(8,128)(2,1)}, bf16[2,128,1024]{2,1,0:T(8,128)(2,1)}, u32[]{:S(2)}, u32[]{:S(2)}) %collective-permute-start.6) | collective-permute-done | bytes 524320 | tf_op jit(solution)/shard_map/ppermute | solution.py:31
  119.5 3.2 %copy-done.3 = bf16[2,2048,1024]{2,1,0:T(8,128)(2,1)} copy-done((bf16[2,2048,1024]{2,1,0:T(8,128)(2,1)}, bf16[2,2048,1024]{2,1,0:T(8,128)(2,1)S(1)}, u32[]{:S(2)}) %copy-start.3) | copy-done | bytes 8388632
  123.5 4.6 %slice.34 = bf16[2,1024,1024]{2,1,0:T(8,128)(2,1)} slice(bf16[3,1024,1024]{2,1,0:T(8,128)(2,1)} %all-gather.2.cloned.1.call-done), slice={[0:2], [0:1024], [0:1024]} | slice | bytes 8388608 | tf_op jit(solution)/shard_map/slice | solution.py:38
  128.1 6.2 %copy.17 = bf16[2,1024,1024]{1,2,0:T(8,128)(2,1)} copy(bf16[2,1024,1024]{2,1,0:T(8,128)(2,1)} %slice.34) | data formatting | bytes 8388608
  134.3 7.4 %convolution_convert_fusion = bf16[1024,2048]{1,0:T(8,128)(2,1)S(1)} fusion(bf16[1024,2048]{0,1:T(8,128)(2,1)} %bitcast.58, bf16[2,2048,1024]{2,1,0:T(8,128)(2,1)} %copy-done.3, s32[]{:T(128)S(6)} %select_n.22), kind=kOutput, calls=%fused_computation.2 | convolution fusion | flops 4297064448 | bytes 10485764 | tf_op jit(solution)/shard_map/dot_general | solution.py:10
  145.0 4.5 %fusion.16 = bf16[1024,128]{1,0:T(8,128)(2,1)S(1)} fusion(bf16[2,2048,1024]{2,1,0:T(8,128)(2,1)} %copy-done.3, s32[]{:T(128)S(6)} %add.38, s32[]{:T(128)S(6)} %select_n.22, bf16[1024,128]{1,0:T(8,128)(2,1)S(1)} %fusion.17, bf16[1024,2048]{1,0:T(8,128)(2,1)} %copy-done.1, bf16[2,1024,128]{2,1,0:T(8,128)(2,1)S(1)} %copy-done.5), kind=kOutput, calls=%fused_computation.19 | convolution fusion | flops 537395200 | bytes 4980744 | tf_op jit(solution)/shard_map/dot_general | solution.py:10
  149.5 8.0 %fusion.3 = bf16[1024,1024]{1,0:T(8,128)(2,1)S(1)} fusion(bf16[3,1024,1024]{2,1,0:T(8,128)(2,1)} %all-gather.2.cloned.1.call-done, bf16[2,2048,1024]{2,1,0:T(8,128)(2,1)} %copy-done.3, s32[]{:T(128)S(6)} %add.38, s32[]{:T(128)S(6)} %select_n.22, bf16[1024,2048]{1,0:T(8,128)(2,1)} %copy-done.1), kind=kOutput, calls=%fused_computation.7 | convolution fusion | flops 4299161600 | bytes 10485768 | tf_op jit(solution)/shard_map/dot_general | solution.py:10
  157.7 2.2 collective-permute-start.8
  160.9 6.1 %collective-permute-start.7 = (bf16[1024,128]{1,0:T(8,128)(2,1)S(1)}, bf16[1024,128]{1,0:T(8,128)(2,1)S(1)}, u32[]{:S(2)}, u32[]{:S(2)}) collective-permute-start(bf16[1024,128]{1,0:T(8,128)(2,1)S(1)} %constant_dynamic-slice_fusion.1), channel_id=1, source_target_pairs={{0,0},{1,1},{2,2},{3,3},{4,4},{5,5},{6,6},{7,7},{8,64},{9,65},{10,... | collective-permute-start | bytes 786440 | tf_op jit(solution)/shard_map/ppermute | solution.py:46
  170.7 37.9 %collective-permute-done.8 = bf16[1024,128]{1,0:T(8,128)(2,1)S(1)} collective-permute-done((bf16[1024,128]{1,0:T(8,128)(2,1)S(1)}, bf16[1024,128]{1,0:T(8,128)(2,1)S(1)}, u32[]{:S(2)}, u32[]{:S(2)}) %collective-permute-start.8) | collective-permute-done | bytes 262176 | tf_op jit(solution)/shard_map/ppermute | solution.py:47
  209.3 4.9 %collective-permute-done.7 = bf16[1024,128]{1,0:T(8,128)(2,1)S(1)} collective-permute-done((bf16[1024,128]{1,0:T(8,128)(2,1)S(1)}, bf16[1024,128]{1,0:T(8,128)(2,1)S(1)}, u32[]{:S(2)}, u32[]{:S(2)}) %collective-permute-start.7) | collective-permute-done | bytes 262176 | tf_op jit(solution)/shard_map/ppermute | solution.py:46
  (50 shorter events, 20.1 us)
Async XLA Ops:
  7.2 109.9 %copy-start = (bf16[2,128,1024]{2,1,0:T(8,128)(2,1)S(1)}, bf16[2,128,1024]{2,1,0:T(8,128)(2,1)}, u32[]{:S(2)}) copy-start(bf16[2,128,1024]{2,1,0:T(8,128)(2,1)} %param.11) | copy-start | bytes 1572868
  7.2 116.3 %all-gather.2.cloned.1.call-start = ((), (), s32[]{:S(2)}) async-start(), calls=%async_computation.1 | async-start | bytes 6389760 | tf_op jit(solution)/shard_map/all_gather | solution.py:37
  26.2 14.6 %collective-permute-start = (bf16[2,128,1024]{2,1,0:T(8,128)(2,1)}, bf16[2,128,1024]{2,1,0:T(8,128)(2,1)S(1)}, u32[]{:S(2)}, u32[]{:S(2)}) collective-permute-start(bf16[2,128,1024]{2,1,0:T(8,128)(2,1)} %param.11), channel_id=1, source_target_pairs={{0,64},{64,128},{128,192},{192,256},{256,320},{320,384},{384,448},... | collective-permute-start | bytes 1572872 | tf_op jit(solution)/shard_map/ppermute | solution.py:31
  40.8 13.6 %collective-permute-start.1 = (bf16[2,128,1024]{2,1,0:T(8,128)(2,1)S(1)}, bf16[2,128,1024]{2,1,0:T(8,128)(2,1)S(1)}, u32[]{:S(2)}, u32[]{:S(2)}) collective-permute-start(bf16[2,128,1024]{2,1,0:T(8,128)(2,1)S(1)} %collective-permute-done), channel_id=1, source_target_pairs={{0,64},{64,128},{128,192},{192,256},{256,320},{320,384},{384,448},... | collective-permute-start | bytes 1572872 | tf_op jit(solution)/shard_map/ppermute | solution.py:31
  54.4 12.7 %collective-permute-start.2 = (bf16[2,128,1024]{2,1,0:T(8,128)(2,1)S(1)}, bf16[2,128,1024]{2,1,0:T(8,128)(2,1)S(1)}, u32[]{:S(2)}, u32[]{:S(2)}) collective-permute-start(bf16[2,128,1024]{2,1,0:T(8,128)(2,1)S(1)} %collective-permute-done.1), channel_id=1, source_target_pairs={{0,64},{64,128},{128,192},{192,256},{256,320},{320,384},{384,448},... | collective-permute-start | bytes 1572872 | tf_op jit(solution)/shard_map/ppermute | solution.py:31
  67.0 11.7 %collective-permute-start.3 = (bf16[2,128,1024]{2,1,0:T(8,128)(2,1)S(1)}, bf16[2,128,1024]{2,1,0:T(8,128)(2,1)S(1)}, u32[]{:S(2)}, u32[]{:S(2)}) collective-permute-start(bf16[2,128,1024]{2,1,0:T(8,128)(2,1)S(1)} %collective-permute-done.2), channel_id=1, source_target_pairs={{0,64},{64,128},{128,192},{192,256},{256,320},{320,384},{384,448},... | collective-permute-start | bytes 1572872 | tf_op jit(solution)/shard_map/ppermute | solution.py:31
  78.8 11.1 %collective-permute-start.4 = (bf16[2,128,1024]{2,1,0:T(8,128)(2,1)S(1)}, bf16[2,128,1024]{2,1,0:T(8,128)(2,1)S(1)}, u32[]{:S(2)}, u32[]{:S(2)}) collective-permute-start(bf16[2,128,1024]{2,1,0:T(8,128)(2,1)S(1)} %collective-permute-done.3), channel_id=1, source_target_pairs={{0,64},{64,128},{128,192},{192,256},{256,320},{320,384},{384,448},... | collective-permute-start | bytes 1572872 | tf_op jit(solution)/shard_map/ppermute | solution.py:31
  89.9 11.9 %collective-permute-start.5 = (bf16[2,128,1024]{2,1,0:T(8,128)(2,1)S(1)}, bf16[2,128,1024]{2,1,0:T(8,128)(2,1)}, u32[]{:S(2)}, u32[]{:S(2)}) collective-permute-start(bf16[2,128,1024]{2,1,0:T(8,128)(2,1)S(1)} %collective-permute-done.4), channel_id=1, source_target_pairs={{0,64},{64,128},{128,192},{192,256},{256,320},{320,384},{384,448},... | collective-permute-start | bytes 1572872 | tf_op jit(solution)/shard_map/ppermute | solution.py:31
  101.8 12.8 %collective-permute-start.6 = (bf16[2,128,1024]{2,1,0:T(8,128)(2,1)}, bf16[2,128,1024]{2,1,0:T(8,128)(2,1)}, u32[]{:S(2)}, u32[]{:S(2)}) collective-permute-start(bf16[2,128,1024]{2,1,0:T(8,128)(2,1)} %collective-permute-done.5), channel_id=1, source_target_pairs={{0,64},{64,128},{128,192},{192,256},{256,320},{320,384},{384,448},... | collective-permute-start | bytes 1572872 | tf_op jit(solution)/shard_map/ppermute | solution.py:31
  116.9 5.9 %copy-start.4 = (bf16[2,1024,128]{2,1,0:T(8,128)(2,1)S(1)}, bf16[2,1024,128]{2,1,0:T(8,128)(2,1)}, u32[]{:S(2)}) copy-start(bf16[2,1024,128]{2,1,0:T(8,128)(2,1)} %param.12) | copy-start | bytes 1572868
  119.5 3.2 %copy-start.3 = (bf16[2,2048,1024]{2,1,0:T(8,128)(2,1)}, bf16[2,2048,1024]{2,1,0:T(8,128)(2,1)S(1)}, u32[]{:S(2)}) copy-start(bf16[2,2048,1024]{2,1,0:T(8,128)(2,1)S(1)} %constant_dynamic-update-slice_fusion) | copy-start | bytes 25165828
  134.3 10.0 %copy-start.6 = (bf16[1024,128]{1,0:T(8,128)(2,1)S(1)}, bf16[1024,128]{1,0:T(8,128)(2,1)}, u32[]{:S(2)}) copy-start(bf16[1024,128]{1,0:T(8,128)(2,1)} %param.13) | copy-start | bytes 786436
  141.7 2.6 %copy-start.1 = (bf16[1024,2048]{1,0:T(8,128)(2,1)}, bf16[1024,2048]{1,0:T(8,128)(2,1)S(1)}, u32[]{:S(2)}) copy-start(bf16[1024,2048]{1,0:T(8,128)(2,1)S(1)} %convolution_convert_fusion) | copy-start | bytes 12582916
  141.7 3.3 %copy-start.5 = (bf16[2,1024,128]{2,1,0:T(8,128)(2,1)S(1)}, bf16[2,1024,128]{2,1,0:T(8,128)(2,1)}, u32[]{:S(2)}) copy-start(bf16[2,1024,128]{2,1,0:T(8,128)(2,1)} %param.12) | copy-start | bytes 1572868
  157.7 56.5 %copy-start.2 = (bf16[1024,2048]{1,0:T(8,128)(2,1)S(1)}, bf16[1024,2048]{1,0:T(8,128)(2,1)}, u32[]{:S(2)}) copy-start(bf16[1024,2048]{1,0:T(8,128)(2,1)} %copy-done.1) | copy-start | bytes 12582916
  157.7 56.5 %copy-start.7 = (bf16[1024,128]{1,0:T(8,128)(2,1)S(1)}, bf16[1024,128]{1,0:T(8,128)(2,1)}, u32[]{:S(2)}) copy-start(bf16[1024,128]{1,0:T(8,128)(2,1)} %param.10) | copy-start | bytes 786436
  157.7 50.9 %collective-permute-start.8 = (bf16[1024,128]{1,0:T(8,128)(2,1)S(1)}, bf16[1024,128]{1,0:T(8,128)(2,1)S(1)}, u32[]{:S(2)}, u32[]{:S(2)}) collective-permute-start(bf16[1024,128]{1,0:T(8,128)(2,1)S(1)} %constant_dynamic-slice_fusion), channel_id=1, source_target_pairs={{0,0},{1,1},{2,2},{3,3},{4,4},{5,5},{6,6},{7,7},{8,64},{9,65},{10,... | collective-permute-start | bytes 786440 | tf_op jit(solution)/shard_map/ppermute | solution.py:47
  160.9 53.3 %collective-permute-start.7 = (bf16[1024,128]{1,0:T(8,128)(2,1)S(1)}, bf16[1024,128]{1,0:T(8,128)(2,1)S(1)}, u32[]{:S(2)}, u32[]{:S(2)}) collective-permute-start(bf16[1024,128]{1,0:T(8,128)(2,1)S(1)} %constant_dynamic-slice_fusion.1), channel_id=1, source_target_pairs={{0,0},{1,1},{2,2},{3,3},{4,4},{5,5},{6,6},{7,7},{8,64},{9,65},{10,... | collective-permute-start | bytes 786440 | tf_op jit(solution)/shard_map/ppermute | solution.py:46
Sparse Core Ops, SparseCore 0:
  26.3 81.5 all-gather.1
